TPU v7x, 128 devices: a whole 4x4x4 slice. The times are simulated.
128 devices in a mesh: req: 32 (over z, x, core), mlp: 4 (over y).
Axes of the slice: x: 4, y: 4, z: 4, core: 2. Of those that a mesh axis runs over, the one named last changes fastest.
Arguments:
- residual_in: bfloat16 [32768, 1664], P('req'), may hold values from -6 to 6
- lengths: int32 [4096], P(('req', 'mlp')), may hold values from 0 to 16, as said below
- owners: int32 [4096], P(('req', 'mlp')), may hold values from 0 to 31, as said below
- merge_dest: int32 [32768], P('req'), may hold values from 0 to 255, as said below
- segment_ids: int32 [32768], P('req'), may hold values from 0 to 3, as said below
- norm2_gain: float32 [1664], replicated, may hold values from 0.5 to 1.5
- norm2_bias: float32 [1664], replicated, may hold values from -3 to 3
- up_weight: bfloat16 [4096, 1664], P('mlp'), may hold values from -0.15625 to 0.15625
- up_bias: float32 [4096], P('mlp'), may hold values from -3 to 3
- down_weight: bfloat16 [4096, 1664], P('mlp'), may hold values from -0.09375 to 0.09375
- down_bias: float32 [1664], replicated, may hold values from -3 to 3
- proj_weight: bfloat16 [6656, 1664], P('mlp'), may hold values from -0.078125 to 0.078125
- norm3_gain: float32 [1664], replicated, may hold values from 0.5 to 1.5
- norm3_bias: float32 [1664], replicated, may hold values from -3 to 3
- next_weight: bfloat16 [1664, 3, 1664], P('req'), may hold values from -0.15625 to 0.15625
Outputs:
- merged_out: bfloat16 [16384, 1664], P(('req', 'mlp'))
- next_mixed: bfloat16 [16384, 1664], P(('req', 'mlp'))
Inputs may be any that keep to these rules, and one draw needn't show every extreme that they name: The 32 pieces of each block of 256 tokens (one device, req-major order) have lengths that are multiples of 4 and sum to 256; in every block one piece has exactly 16 tokens. The owners of the 32 pieces of one block are a permutation of 0 to 31; for each index of mlp, one piece of 16 tokens of each block of that index goes to one owner shared by all blocks of that index. `merge_dest`: within each device block a permutation of 0 to 255 that maps the tokens of each piece onto that piece's own positions. `segment_ids`: the four tokens of a block whose merge_dest values have the same quotient by 4 carry one segment id.
All inputs are finite; a program needn't handle non-finite values.
Results may differ from a plain program's by a relative error of at most 0.023.
Values may be sent and summed in bfloat16 or wider, within the bound.
No kernel may reach another device: no remote copies, remote signals or barrier semaphores. Data moves between devices by JAX's collectives and lax.ppermute only.
A program may use at most 128 MiB of HBM per device.

v0:
```python
import math
import jax
import jax.numpy as jnp
from jax import lax
from jax.sharding import PartitionSpec as P

HEAD_DIM = 104
EPSILON = 1e-06


def layer_norm(rows, gain, bias):
    values = rows.astype(jnp.float32)
    mean_value = jnp.mean(values, axis=-1, keepdims=True)
    centred = values - mean_value
    spread = jnp.mean(centred * centred, axis=-1, keepdims=True)
    return centred * lax.rsqrt(spread + EPSILON) * gain + bias


def block_attention(heads_in, slot_tags):
    queries = heads_in[:, :, 0]
    key_rows = heads_in[:, :, 1]
    value_rows = heads_in[:, :, 2]
    score_scale = 1.0 / math.sqrt(heads_in.shape[-1])
    scores = (
        jnp.einsum("bqhe,bkhe->bhqk", queries, key_rows, preferred_element_type=jnp.float32)
        * score_scale
    )
    slot_total = heads_in.shape[1]
    itself = lax.broadcasted_iota(jnp.int32, (slot_total, slot_total), 0) == lax.broadcasted_iota(
        jnp.int32, (slot_total, slot_total), 1
    )
    live_slots = slot_tags >= 0
    same_request = slot_tags[:, :, None] == slot_tags[:, None, :]
    allowed = same_request & live_slots[:, None, :] | itself[None]
    weights = jnp.where(allowed[:, None], jnp.exp(scores), 0.0)
    probs = (weights / jnp.sum(weights, axis=-1, keepdims=True)).astype(jnp.bfloat16)
    mixed_out = jnp.einsum("bhqk,bkhe->bqhe", probs, value_rows, preferred_element_type=jnp.float32)
    mixed_out = jnp.where(live_slots[:, :, None, None], mixed_out, 0.0)
    return mixed_out.astype(jnp.bfloat16)


def body(
    residual_in,
    lengths,
    owners,
    merge_dest,
    segment_ids,
    norm2_gain,
    norm2_bias,
    up_weight,
    up_bias,
    down_weight,
    down_bias,
    proj_weight,
    norm3_gain,
    norm3_bias,
    next_weight,
):
    group_rows, model_width = residual_in.shape
    lane_count = lax.axis_size("mlp")
    sender_count = lax.axis_size("req")
    lane_index = lax.axis_index("mlp")
    own_rows = group_rows // lane_count
    merged_rows = own_rows // 4
    slot_count = 2 * merged_rows // sender_count
    normed = layer_norm(residual_in, norm2_gain, norm2_bias).astype(jnp.bfloat16)
    upward = lax.dot_general(
        normed, up_weight, (((1,), (1,)), ((), ())), preferred_element_type=jnp.float32
    )
    hidden = jax.nn.gelu(upward + up_bias, approximate=False).astype(jnp.bfloat16)
    partial_sums = jnp.dot(hidden, down_weight, preferred_element_type=jnp.float32)
    places = merge_dest.reshape(lane_count, own_rows)
    block_ids = lax.broadcasted_iota(jnp.int32, (lane_count, own_rows), 0)
    token_ids = lax.broadcasted_iota(jnp.int32, (lane_count, own_rows), 1)
    sources = jnp.zeros((lane_count, own_rows), jnp.int32).at[block_ids, places].set(token_ids)
    block_offset = own_rows * lax.broadcasted_iota(jnp.int32, (lane_count, merged_rows, 4), 0)
    group_index = sources.reshape(lane_count, merged_rows, 4) + block_offset
    quadrant_rows = lax.dynamic_index_in_dim(group_index, lane_index, 2, False).reshape(-1)
    feed_out = lax.psum(partial_sums.astype(jnp.bfloat16), "mlp").astype(jnp.float32)
    layer_out = (residual_in.astype(jnp.float32) + feed_out + down_bias).astype(jnp.bfloat16)
    quarter = jnp.take(layer_out, quadrant_rows, axis=0)
    projected = lax.psum_scatter(
        jnp.dot(quarter, proj_weight, preferred_element_type=jnp.float32).astype(jnp.bfloat16),
        "mlp",
        scatter_dimension=0,
        tiled=True,
    )
    first_tokens = lax.dynamic_index_in_dim(group_index[:, :, 0], lane_index, 0, False)
    row_segment = jnp.take(segment_ids, first_tokens, axis=0)
    counts = lengths // 4
    starts = jnp.cumsum(counts) - counts
    index = lax.broadcasted_iota(jnp.int32, (merged_rows, 1), 0)
    inside = ((index >= starts[None, :]) & (index < (starts + counts)[None, :])).astype(jnp.int32)
    owner_of = jnp.sum(inside * owners[None, :], axis=1)
    rank = index[:, 0] - jnp.sum(inside * starts[None, :], axis=1)
    target = owner_of * slot_count + rank
    slot_ids = lax.broadcasted_iota(jnp.int32, (sender_count * slot_count, 1), 0)
    route_hits = slot_ids == target[None, :]
    outgoing = jnp.dot(
        route_hits.astype(jnp.bfloat16), projected, preferred_element_type=jnp.float32
    ).astype(jnp.bfloat16)
    sent_tags = jnp.sum(route_hits.astype(jnp.int32) * (row_segment + 1)[None, :], axis=1) - 1
    received, arrived_tags = (
        lax.all_to_all(outgoing, "req", split_axis=0, concat_axis=0, tiled=True),
        lax.all_to_all(sent_tags, "req", split_axis=0, concat_axis=0, tiled=True),
    )
    normed3 = layer_norm(received, norm3_gain, norm3_bias).astype(jnp.bfloat16)
    recv_rows = received.shape[0]
    piece = lax.all_gather(next_weight, "req", axis=0, tiled=True)
    heads_in = jnp.dot(
        normed3, piece.reshape(piece.shape[0], -1), preferred_element_type=jnp.float32
    )
    heads_in = heads_in.astype(jnp.bfloat16).reshape(1, recv_rows, 3, -1, HEAD_DIM)
    next_mixed = block_attention(heads_in, arrived_tags.reshape(1, recv_rows)).reshape(
        recv_rows, model_width
    )
    return (received, next_mixed)


def solution(mesh):
    return jax.shard_map(
        body,
        mesh=mesh,
        in_specs=(
            P("req", None),
            P(("req", "mlp")),
            P(("req", "mlp")),
            P("req"),
            P("req"),
            P(),
            P(),
            P("mlp", None),
            P("mlp"),
            P("mlp", None),
            P(),
            P("mlp", None),
            P(),
            P(),
            P("req", None, None),
        ),
        out_specs=(P(("req", "mlp"), None), P(("req", "mlp"), None)),
        check_vma=False,
    )
```

profile of v0, /device:TPU:1, one launch (start us, length us, event | category | flops | bytes accessed | tf_op | source)
XLA Modules:
  0.0 286.2 jit_solution(13230346240546526583)
XLA Ops:
  8.0 0.0 copy-start
  8.0 0.0 all-reduce.2.cloned.1.call-start
  8.1 0.0 copy-start.3
  8.1 2.6 convert_reduce_fusion
  10.8 0.5 copy-done.3
  11.2 1.0 fusion.2
  12.3 0.0 copy-start.9
  12.3 0.0 copy-start.12
  12.3 0.0 copy-start.11
  12.3 20.5 %convolution_convert_fusion.1 = bf16[1024,1664]{1,0:T(8,128)(2,1)} fusion(bf16[1024,1664]{1,0:T(8,128)(2,1)S(1)} %copy-done, bf16[1024,1664]{1,0:T(8,128)(2,1)} %param.22, bf16[1024,1664]{1,0:T(8,128)(2,1)} %param.15, f32[1664]{0:T(1024)S(1)} %copy-done.13, f32[1664]{0:T(1024)S(1)} %copy-done.14, f32[1024]{0:T(1024)S(1)} %add_rsqrt_fusion.1, ...), kind=kOutput, calls=%fused_computation.34 | convolution fusion | flops 7060455424 | bytes 13657088 | tf_op jit(solution)/shard_map/dot_general | solution.py:71
  32.9 0.0 all-reduce.2.cloned.1.call-update
  32.9 0.0 reduce-scatter.2.cloned.1.call-start
  33.0 0.1 multiply_reduce_fusion
  33.1 0.1 and_reduce_fusion
  33.2 4.5 %scatter_custom_fusion = s32[1024]{0:T(1024)S(1)} fusion(s32[1024]{0:T(1024)S(1)} %bitcast.53, s32[1024]{0:T(1024)S(1)} %bitcast.54, s32[]{:T(128)} %constant.46.clone.1), kind=kCustom, calls=%fused_computation.124 | custom fusion | bytes 4100
  37.7 0.1 reshape.396
  37.8 0.1 broadcast_add_fusion
  37.9 0.2 fusion.116
  38.2 0.1 reshape.398
  38.2 0.7 reshape.397
  38.9 0.7 compare_and_fusion
  39.6 76.7 %all-reduce.2.cloned.1.call-done = bf16[1024,1664]{1,0:T(8,128)(2,1)} async-done(((bf16[1024,1664]{1,0:T(8,128)(2,1)}), bf16[1024,1664]{1,0:T(8,128)(2,1)}) %all-reduce.2.cloned.1.call-update) | async-done | bytes 3407888 | tf_op jit(solution)/shard_map/psum | solution.py:79
  116.3 0.0 copy-done.4
  116.3 4.8 %fusion.7 = bf16[1024,1664]{1,0:T(8,128)(2,1)} fusion(bf16[1024,1664]{1,0:T(8,128)(2,1)S(1)} %copy-done.4, bf16[1024,1664]{1,0:T(8,128)(2,1)} %all-reduce.2.cloned.1.call-done, f32[1664]{0:T(1024)S(1)} %copy-done.8), kind=kLoop, calls=%fused_computation.13 | loop fusion | flops 8519680 | bytes 10230272 | tf_op jit(solution)/shard_map/convert_element_type | solution.py:80
  121.1 4.5 %gather_fusion = bf16[256,1664]{1,0:T(8,128)(2,1)S(1)} fusion(bf16[1024,1664]{1,0:T(8,128)(2,1)} %fusion.7, s32[1024]{0:T(1024)S(1)} %pad_clamp_fusion.1), kind=kCustom, calls=%fused_computation | custom fusion | bytes 1704960 | tf_op jit(solution)/shard_map/jit(_take)/gather | solution.py:81
  125.6 0.0 copy-start.5
  125.6 0.0 copy-start.16
  125.7 0.0 copy-start.2
  125.7 0.0 copy-start.10
  125.7 5.5 %convolution_convert_fusion.2 = bf16[256,1664]{1,0:T(8,128)(2,1)} fusion(bf16[1664,1664]{1,0:T(8,128)(2,1)} %param.26, bf16[256,1664]{1,0:T(8,128)(2,1)S(1)} %gather_fusion, pred[256]{0:T(512)(128)(4,1)S(1)} %compare_and_fusion), kind=kOutput, calls=%fused_computation.40 | convolution fusion | flops 1418526720 | bytes 7241984 | tf_op jit(solution)/shard_map/dot_general | solution.py:83
  131.2 0.0 reduce-scatter.2.cloned.1.call-update
  131.2 0.0 all-gather.2.cloned.1.call-start
  131.2 1.1 copy.42
  132.4 0.0 all-gather.2.cloned.1.call-update
  132.4 0.1 copy.40
  132.5 0.1 reduce-window.8
  132.6 0.1 reduce.6
  132.7 0.1 dynamic-slice_reduce_fusion.1
  132.8 0.7 gather_fusion.1
  133.6 0.1 select_reduce_fusion.2
  133.7 0.1 select_reduce_fusion
  133.8 0.1 sub.46
  133.9 14.4 %all_to_all.21 = s32[32,4,1]{1,2,0:T(1,128)S(1)} all-to-all(s32[32,4,1]{1,2,0:T(1,128)S(1)} %bitcast.51), channel_id=1, replica_groups=mesh['req'=32,'mlp'=4] {'req'}, dimensions={0} | all-to-all | bytes 1024 | tf_op jit(solution)/shard_map/all_to_all | solution.py:105
  148.3 0.5 broadcast.328
  148.8 0.7 reduce.18
  149.5 0.1 all_to_all.18
  149.6 3.1 %reduce-scatter.2.cloned.1.call-done = bf16[64,1664]{1,0:T(8,128)(2,1)} async-done(((bf16[256,1664]{1,0:T(8,128)(2,1)}), bf16[64,1664]{1,0:T(8,128)(2,1)}) %reduce-scatter.2.cloned.1.call-update) | async-done | bytes 213008 | tf_op jit(solution)/shard_map/reduce_scatter | solution.py:82
  152.7 1.3 convolution_convert_fusion.3
  154.0 0.9 all_to_all.14
  154.9 8.8 %all-to-all-start = ((bf16[32,4,1664]{2,1,0:T(4,128)(2,1)}), bf16[32,4,1664]{2,1,0:T(4,128)(2,1)S(1)}, u32[]{:S(2)}, u32[]{:S(2)}) async-start(bf16[32,4,1664]{2,1,0:T(4,128)(2,1)} %all_to_all.14), calls=%async_computation.1 | async-start | bytes 851968 | tf_op jit(solution)/shard_map/all_to_all | solution.py:104
  163.7 0.1 fusion.74
  163.9 10.4 %all-to-all-done = bf16[32,4,1664]{2,1,0:T(4,128)(2,1)S(1)} async-done(((bf16[32,4,1664]{2,1,0:T(4,128)(2,1)}), bf16[32,4,1664]{2,1,0:T(4,128)(2,1)S(1)}, u32[]{:S(2)}, u32[]{:S(2)}) %all-to-all-start) | async-done | bytes 426016 | tf_op jit(solution)/shard_map/all_to_all | solution.py:104
  174.3 0.2 convert_reduce_fusion.1
  174.5 0.4 fusion.65
  175.0 0.4 fusion.68
  175.4 0.1 convert_element_type.63
  175.5 0.9 all_to_all.16
  176.4 44.4 %all-gather.2.cloned.1.call-done = bf16[1664,3,1664]{2,1,0:T(4,128)(2,1)} async-done(((bf16[52,3,1664]{2,1,0:T(4,128)(2,1)}), bf16[1664,3,1664]{2,1,0:T(4,128)(2,1)}) %all-gather.2.cloned.1.call-update) | async-done | bytes 16613392 | tf_op jit(solution)/shard_map/all_gather | solution.py:109
  220.8 36.4 %copy.43 = bf16[1664,3,1664]{0,2,1:T(8,128)(2,1)} copy(bf16[1664,3,1664]{2,1,0:T(4,128)(2,1)} %all-gather.2.cloned.1.call-done) | data formatting | bytes 33226752 | tf_op jit(solution)/shard_map/all_gather | solution.py:109
  257.2 11.7 %convolution_convert_fusion = bf16[128,4992]{1,0:T(8,128)(2,1)} fusion(bf16[128,1664]{1,0:T(8,128)(2,1)S(1)} %convert_element_type.63, bf16[1664,4992]{0,1:T(8,128)(2,1)} %bitcast.47), kind=kOutput, calls=%fused_computation.15 | convolution fusion | flops 2127151104 | bytes 18317312 | tf_op jit(solution)/shard_map/dot_general | solution.py:110
  268.8 2.6 copy.44
  271.4 2.5 fusion.60
  273.9 2.8 fusion.62
  276.8 2.0 copy.46
  (45 shorter events, 0.2 us)
Async XLA Ops:
  8.0 4.3 %copy-start = (bf16[1024,1664]{1,0:T(8,128)(2,1)S(1)}, bf16[1024,1664]{1,0:T(8,128)(2,1)}, u32[]{:S(2)}) copy-start(bf16[1024,1664]{1,0:T(8,128)(2,1)} %param.24) | copy-start | bytes 10223620
  8.0 4.3 %copy-start.15 = (f32[1024]{0:T(1024)S(1)}, f32[1024]{0:T(1024)}, u32[]{:S(2)}) copy-start(f32[1024]{0:T(1024)} %param.23) | copy-start | bytes 12292
  8.0 4.3 %copy-start.13 = (f32[1664]{0:T(1024)S(1)}, f32[1664]{0:T(1024)}, u32[]{:S(2)}) copy-start(f32[1664]{0:T(1024)} %param.21) | copy-start | bytes 19972
  8.0 108.3 %all-reduce.2.cloned.1.call-start = ((), (), s32[]{:S(2)}) async-start(), calls=%async_computation.3 | async-start | bytes 6815744 | tf_op jit(solution)/shard_map/psum | solution.py:79
  8.1 3.1 %copy-start.3 = (bf16[1024,1664]{1,0:T(8,128)(2,1)S(1)}, bf16[1024,1664]{1,0:T(8,128)(2,1)}, u32[]{:S(2)}) copy-start(bf16[1024,1664]{1,0:T(8,128)(2,1)} %param.15) | copy-start | bytes 10223620
  8.1 4.2 %copy-start.14 = (f32[1664]{0:T(1024)S(1)}, f32[1664]{0:T(1024)}, u32[]{:S(2)}) copy-start(f32[1664]{0:T(1024)} %param.20) | copy-start | bytes 19972
  12.3 20.6 %copy-start.9 = (s32[1024]{0:T(1024)S(1)}, s32[1024]{0:T(1024)}, u32[]{:S(2)}) copy-start(s32[1024]{0:T(1024)} %param.18) | copy-start | bytes 12292
  12.3 20.7 %copy-start.12 = (s32[2]{0:T(128)S(1)}, s32[2]{0:T(128)}, u32[]{:S(2)}) copy-start(s32[2]{0:T(128)} %constant.153) | copy-start | bytes 28
  12.3 20.7 %copy-start.11 = (s32[2]{0:T(128)S(1)}, s32[2]{0:T(128)}, u32[]{:S(2)}) copy-start(s32[2]{0:T(128)} %constant.156) | copy-start | bytes 28
  32.9 83.4 %copy-start.4 = (bf16[1024,1664]{1,0:T(8,128)(2,1)S(1)}, bf16[1024,1664]{1,0:T(8,128)(2,1)}, u32[]{:S(2)}) copy-start(bf16[1024,1664]{1,0:T(8,128)(2,1)} %param.15) | copy-start | bytes 10223620
  32.9 83.4 %copy-start.8 = (f32[1664]{0:T(1024)S(1)}, f32[1664]{0:T(1024)}, u32[]{:S(2)}) copy-start(f32[1664]{0:T(1024)} %param.25) | copy-start | bytes 19972
  32.9 119.8 %reduce-scatter.2.cloned.1.call-start = ((), (), s32[]{:S(2)}) async-start(), calls=%async_computation.4 | async-start | bytes 1064960 | tf_op jit(solution)/shard_map/reduce_scatter | solution.py:82
  125.6 5.6 %copy-start.5 = (bf16[52,3,1664]{2,0,1:T(8,128)(2,1)S(1)}, bf16[52,3,1664]{2,0,1:T(8,128)(2,1)}, u32[]{:S(2)}) copy-start(bf16[52,3,1664]{2,0,1:T(8,128)(2,1)} %param.29) | copy-start | bytes 1557508
  125.6 6.8 %copy-start.16 = (s32[32]{0:T(128)S(1)}, s32[32]{0:T(128)}, u32[]{:S(2)}) copy-start(s32[32]{0:T(128)} %param.16) | copy-start | bytes 388
  125.7 7.2 %copy-start.2 = (s32[1024]{0:T(1024)S(1)}, s32[1024]{0:T(1024)}, u32[]{:S(2)}) copy-start(s32[1024]{0:T(1024)} %param.19) | copy-start | bytes 12292
  125.7 7.9 %copy-start.10 = (s32[32]{0:T(128)S(1)}, s32[32]{0:T(128)}, u32[]{:S(2)}) copy-start(s32[32]{0:T(128)} %param.17) | copy-start | bytes 388
  131.2 43.8 %copy-start.6 = (f32[1664]{0:T(1024)S(1)}, f32[1664]{0:T(1024)}, u32[]{:S(2)}) copy-start(f32[1664]{0:T(1024)} %param.28) | copy-start | bytes 19972
  131.2 43.8 %copy-start.7 = (f32[1664]{0:T(1024)S(1)}, f32[1664]{0:T(1024)}, u32[]{:S(2)}) copy-start(f32[1664]{0:T(1024)} %param.27) | copy-start | bytes 19972
  131.2 89.6 %all-gather.2.cloned.1.call-start = ((), (), s32[]{:S(2)}) async-start(), calls=%async_computation.5 | async-start | bytes 22843392 | tf_op jit(solution)/shard_map/all_gather | solution.py:109
  154.9 19.4 %all-to-all-start = ((bf16[32,4,1664]{2,1,0:T(4,128)(2,1)}), bf16[32,4,1664]{2,1,0:T(4,128)(2,1)S(1)}, u32[]{:S(2)}, u32[]{:S(2)}) async-start(bf16[32,4,1664]{2,1,0:T(4,128)(2,1)} %all_to_all.14), calls=%async_computation.1 | async-start | bytes 851968 | tf_op jit(solution)/shard_map/all_to_all | solution.py:104
  268.8 9.9 %copy-start.1 = (bf16[1024,1664]{1,0:T(8,128)(2,1)S(1)}, bf16[1024,1664]{1,0:T(8,128)(2,1)}, u32[]{:S(2)}) copy-start(bf16[1024,1664]{1,0:T(8,128)(2,1)} %param.24) | copy-start | bytes 10223620
Sparse Core Ops, SparseCore 0:
  33.0 83.2 all-reduce.1
  131.3 21.3 reduce-scatter.1
Sparse Core Ops, SparseCore 1:
  134.3 86.4 all-gather.1
where the time goes:
time: 288 us; the launch traced here: 286 us
  waiting for transfers between devices  135 us (47%)
  local copies, waits for them, and re-layouts  56.2 us (20%)
  matrix products  44.3 us (15%)
  between operations  15.9 us (6%)
  blocking collectives  14.4 us (5%)
  other arithmetic  11.7 us (4%)
  starting transfers between devices  8.95 us (3%)
    psum x1, waiting for transfers between devices, body(): lax.psum(partial_sums.astype(jnp.bfloat16), 'mlp').astype(jnp.float32)  76.7 us
    all_gather x1, waiting for transfers between devices, body(): piece = lax.all_gather(next_weight, 'req', axis=0, tiled=True)  44.4 us
    all_gather x1, local copies, waits for them, and re-layouts, body(): piece = lax.all_gather(next_weight, 'req', axis=0, tiled=True)  36.4 us
    dot_general x1, matrix products, body(): jnp.dot(hidden, down_weight, preferred_element_type=jnp.float32)  20.5 us
    all_to_all x1, blocking collectives, body(): lax.all_to_all(sent_tags, 'req', split_axis=0, concat_axis=0, tiled=True)  14.4 us
    dot_general x1, matrix products, body(): jnp.dot(normed3, piece.reshape(piece.shape[0], -1), preferred_element_typ...  11.7 us
    all_to_all x1, waiting for transfers between devices, body(): lax.all_to_all(outgoing, 'req', split_axis=0, concat_axis=0, tiled=True)  10.4 us
    all_to_all x1, starting transfers between devices, body(): lax.all_to_all(outgoing, 'req', split_axis=0, concat_axis=0, tiled=True)  8.83 us
  transfers between devices with their start and end apart: 4, of which 4 were waited for; matrix products, arithmetic and copies ran while one was open for 5% of the time, Pallas kernels for 0%

commit v1 on v0

--- a/solution.py
+++ b/solution.py
@@ -56,6 +56,14 @@
     norm3_bias,
     next_weight,
 ):
+
+    def link_space(array_in):
+        inter = jax.lax.all_to_all(
+            jnp.stack(jax.lax.axis_size("req") * [array_in], axis=0), "req", 0, 0
+        )
+        f_next = jnp.concatenate(inter, axis=0)
+        return f_next
+
     group_rows, model_width = residual_in.shape
     lane_count = lax.axis_size("mlp")
     sender_count = lax.axis_size("req")
@@ -106,7 +114,7 @@
     )
     normed3 = layer_norm(received, norm3_gain, norm3_bias).astype(jnp.bfloat16)
     recv_rows = received.shape[0]
-    piece = lax.all_gather(next_weight, "req", axis=0, tiled=True)
+    piece = link_space(next_weight)
     heads_in = jnp.dot(
         normed3, piece.reshape(piece.shape[0], -1), preferred_element_type=jnp.float32
     )

time: 288 us -> 482 us (1.67)
  the two profiles are of different devices: /device:TPU:1 before, /device:TPU:0 now
where the time goes in v1:
time: 482 us; the launch traced here: 481 us
  waiting for transfers between devices  314 us (65%)
  local copies, waits for them, and re-layouts  74.5 us (15%)
  matrix products  36.4 us (8%)
  blocking collectives  17.7 us (4%)
  between operations  14.4 us (3%)
  starting transfers between devices  12.9 us (3%)
  other arithmetic  11.7 us (2%)
    all_to_all x1, waiting for transfers between devices, link_space(): jax.lax.all_to_all(jnp.stack(jax.lax.axis_size('req') * [array_in], axis=...  224 us
    psum x1, waiting for transfers between devices, body(): lax.psum(partial_sums.astype(jnp.bfloat16), 'mlp').astype(jnp.float32)  75.9 us
    all_to_all x1, local copies, waits for them, and re-layouts, link_space(): jax.lax.all_to_all(jnp.stack(jax.lax.axis_size('req') * [array_in], axis=...  37.1 us
    dot_general x1, matrix products, body(): jnp.dot(hidden, down_weight, preferred_element_type=jnp.float32)  20.5 us
    unnamed x40, local copies, waits for them, and re-layouts  19.5 us
    all_to_all x1, blocking collectives, body(): lax.all_to_all(outgoing, 'req', split_axis=0, concat_axis=0, tiled=True)  17.7 us
    reduce_scatter x1, waiting for transfers between devices, body(): lax.psum_scatter(jnp.dot(quarter, proj_weight, preferred_element_type=jnp...  13.3 us
  transfers between devices with their start and end apart: 4, of which 3 were waited for; matrix products, arithmetic and copies ran while one was open for 3% of the time, Pallas kernels for 0%

profile of v1, /device:TPU:0, one launch (start us, length us, event | category | flops | bytes accessed | tf_op | source)
XLA Modules:
  0.0 481.2 jit_solution(10664085879074266490)
XLA Ops:
  7.2 0.0 copy-start
  7.2 0.0 all-reduce.2.cloned.1.call-start
  7.2 0.0 copy-start.3
  7.3 2.6 convert_reduce_fusion
  9.9 0.5 copy-done.3
  10.4 1.0 fusion.2
  11.5 0.0 copy-start.9
  11.5 0.0 copy-start.12
  11.5 0.0 copy-start.11
  11.5 20.5 %convolution_convert_fusion.1 = bf16[1024,1664]{1,0:T(8,128)(2,1)} fusion(bf16[1024,1664]{1,0:T(8,128)(2,1)S(1)} %copy-done, bf16[1024,1664]{1,0:T(8,128)(2,1)} %param.22, bf16[1024,1664]{1,0:T(8,128)(2,1)} %param.15, f32[1664]{0:T(1024)S(1)} %copy-done.13, f32[1664]{0:T(1024)S(1)} %copy-done.14, f32[1024]{0:T(1024)S(1)} %add_rsqrt_fusion.1, ...), kind=kOutput, calls=%fused_computation.34 | convolution fusion | flops 7060455424 | bytes 13657088 | tf_op jit(solution)/shard_map/dot_general | solution.py:79
  32.0 0.0 all-reduce.2.cloned.1.call-update
  32.0 0.0 reduce-scatter.2.cloned.1.call-start
  32.1 0.0 copy-done.9
  32.2 0.1 multiply_reduce_fusion
  32.2 0.1 and_reduce_fusion
  32.4 4.5 scatter_custom_fusion
  36.9 0.1 reshape.395
  37.0 0.1 broadcast_add_fusion
  37.1 0.2 fusion.116
  37.3 0.1 reshape.397
  37.4 0.7 reshape.396
  38.1 0.7 compare_and_fusion
  38.8 75.9 %all-reduce.2.cloned.1.call-done = bf16[1024,1664]{1,0:T(8,128)(2,1)} async-done(((bf16[1024,1664]{1,0:T(8,128)(2,1)}), bf16[1024,1664]{1,0:T(8,128)(2,1)}) %all-reduce.2.cloned.1.call-update) | async-done | bytes 3407888 | tf_op jit(solution)/shard_map/psum | solution.py:87
  114.7 4.8 fusion.7
  119.5 4.5 gather_fusion
  124.0 0.0 copy-start.16
  124.1 0.0 copy-start.2
  124.1 0.0 copy-start.10
  124.1 5.4 %convolution_convert_fusion.2 = bf16[256,1664]{1,0:T(8,128)(2,1)} fusion(bf16[1664,1664]{1,0:T(8,128)(2,1)} %param.26, bf16[256,1664]{1,0:T(8,128)(2,1)S(1)} %gather_fusion, pred[256]{0:T(512)(128)(4,1)S(1)} %compare_and_fusion), kind=kOutput, calls=%fused_computation.40 | convolution fusion | flops 1418526720 | bytes 7241984 | tf_op jit(solution)/shard_map/dot_general | solution.py:91
  129.5 0.0 reduce-scatter.2.cloned.1.call-update
  129.5 0.0 copy-done.16
  129.5 0.1 copy.40
  129.6 0.1 reduce-window.8
  129.7 0.1 reduce.6
  129.8 0.1 dynamic-slice_reduce_fusion.1
  129.9 0.7 gather_fusion.1
  130.7 0.1 select_reduce_fusion.2
  130.8 0.1 select_reduce_fusion
  130.9 0.7 sub.46
  131.6 7.2 %all-to-all-start.1 = ((s32[32,4,1]{1,2,0:T(1,128)}), s32[32,4,1]{1,2,0:T(1,128)S(1)}, u32[]{:S(2)}, u32[]{:S(2)}) async-start(s32[32,4,1]{1,2,0:T(1,128)} %bitcast.3), calls=%async_computation.2 | async-start | bytes 32768 | tf_op jit(solution)/shard_map/all_to_all | solution.py:113
  138.9 13.3 %reduce-scatter.2.cloned.1.call-done = bf16[64,1664]{1,0:T(8,128)(2,1)} async-done(((bf16[256,1664]{1,0:T(8,128)(2,1)}), bf16[64,1664]{1,0:T(8,128)(2,1)}) %reduce-scatter.2.cloned.1.call-update) | async-done | bytes 213008 | tf_op jit(solution)/shard_map/reduce_scatter | solution.py:90
  152.2 1.3 convolution_convert_fusion.3
  153.5 0.1 all_to_all.17
  153.6 0.0 all-to-all-done.1
  153.6 17.7 %all_to_all.26 = bf16[32,4,1664]{2,1,0:T(4,128)(2,1)S(1)} all-to-all(bf16[32,4,1664]{2,1,0:T(4,128)(2,1)S(1)} %all_to_all.17), channel_id=1, replica_groups=mesh['req'=32,'mlp'=4] {'req'}, dimensions={0} | all-to-all | bytes 851968 | tf_op jit(solution)/shard_map/all_to_all | solution.py:112
  171.3 6.3 %stack.2 = bf16[32,52,3,1664]{3,1,2,0:T(8,128)(2,1)} broadcast(bf16[52,3,1664]{2,0,1:T(8,128)(2,1)S(1)} %copy-done.5), dimensions={1,2,3} | broadcast | bytes 17132544 | tf_op jit(solution)/shard_map/stack | solution.py:62
  177.6 5.6 %all-to-all-start.2 = ((bf16[32,52,3,1664]{3,1,2,0:T(8,128)(2,1)}), bf16[32,52,3,1664]{3,1,2,0:T(8,128)(2,1)}, u32[]{:S(2)}, u32[]{:S(2)}) async-start(bf16[32,52,3,1664]{3,1,2,0:T(8,128)(2,1)} %stack.2), calls=%async_computation.3 | async-start | bytes 35782656 | tf_op jit(solution)/shard_map/all_to_all | solution.py:61
  183.2 0.5 broadcast.330
  183.7 0.7 reduce.18
  184.4 0.1 all_to_all.21
  184.5 0.1 fusion.74
  184.6 0.2 convert_reduce_fusion.1
  184.9 0.4 fusion.65
  185.3 0.4 fusion.68
  185.7 0.1 convert_element_type.63
  185.8 0.9 all_to_all.19
  186.7 224.4 %all-to-all-done.2 = bf16[32,52,3,1664]{3,1,2,0:T(8,128)(2,1)} async-done(((bf16[32,52,3,1664]{3,1,2,0:T(8,128)(2,1)}), bf16[32,52,3,1664]{3,1,2,0:T(8,128)(2,1)}, u32[]{:S(2)}, u32[]{:S(2)}) %all-to-all-start.2) | async-done | bytes 16613408 | tf_op jit(solution)/shard_map/all_to_all | solution.py:61
  411.1 37.1 %copy.42 = bf16[32,52,3,1664]{3,2,1,0:T(4,128)(2,1)} copy(bf16[32,52,3,1664]{3,1,2,0:T(8,128)(2,1)} %all-to-all-done.2) | data formatting | bytes 33226752 | tf_op jit(solution)/shard_map/all_to_all | solution.py:61
  448.2 12.5 %copy.49 = bf16[208,8,3,1664]{3,1,2,0:T(8,128)(2,1)S(1)} copy(bf16[208,8,3,1664]{3,2,1,0:T(4,128)(2,1)} %bitcast.49) | data formatting | bytes 33226752
  460.7 3.7 convolution_convert_fusion
  464.4 2.6 copy.43
  467.0 2.5 fusion.60
  469.5 2.9 fusion.62
  472.4 2.0 copy.45
  (45 shorter events, 0.2 us)
Async XLA Ops:
  7.2 4.3 copy-start
  7.2 4.3 copy-start.15
  7.2 4.3 copy-start.13
  7.2 107.5 %all-reduce.2.cloned.1.call-start = ((), (), s32[]{:S(2)}) async-start(), calls=%async_computation.4 | async-start | bytes 6815744 | tf_op jit(solution)/shard_map/psum | solution.py:87
  7.2 3.1 copy-start.3
  7.3 4.2 copy-start.14
  11.5 20.6 %copy-start.9 = (s32[1024]{0:T(1024)S(1)}, s32[1024]{0:T(1024)}, u32[]{:S(2)}) copy-start(s32[1024]{0:T(1024)} %param.18) | copy-start | bytes 12292
  11.5 20.7 %copy-start.12 = (s32[2]{0:T(128)S(1)}, s32[2]{0:T(128)}, u32[]{:S(2)}) copy-start(s32[2]{0:T(128)} %constant.153) | copy-start | bytes 28
  11.5 20.7 %copy-start.11 = (s32[2]{0:T(128)S(1)}, s32[2]{0:T(128)}, u32[]{:S(2)}) copy-start(s32[2]{0:T(128)} %constant.156) | copy-start | bytes 28
  32.0 82.7 %copy-start.4 = (bf16[1024,1664]{1,0:T(8,128)(2,1)S(1)}, bf16[1024,1664]{1,0:T(8,128)(2,1)}, u32[]{:S(2)}) copy-start(bf16[1024,1664]{1,0:T(8,128)(2,1)} %param.15) | copy-start | bytes 10223620
  32.0 82.7 %copy-start.8 = (f32[1664]{0:T(1024)S(1)}, f32[1664]{0:T(1024)}, u32[]{:S(2)}) copy-start(f32[1664]{0:T(1024)} %param.25) | copy-start | bytes 19972
  32.0 120.1 %reduce-scatter.2.cloned.1.call-start = ((), (), s32[]{:S(2)}) async-start(), calls=%async_computation.5 | async-start | bytes 1064960 | tf_op jit(solution)/shard_map/reduce_scatter | solution.py:90
  124.0 5.5 %copy-start.16 = (s32[32]{0:T(128)S(1)}, s32[32]{0:T(128)}, u32[]{:S(2)}) copy-start(s32[32]{0:T(128)} %param.16) | copy-start | bytes 388
  124.1 5.9 %copy-start.2 = (s32[1024]{0:T(1024)S(1)}, s32[1024]{0:T(1024)}, u32[]{:S(2)}) copy-start(s32[1024]{0:T(1024)} %param.19) | copy-start | bytes 12292
  124.1 6.6 %copy-start.10 = (s32[32]{0:T(128)S(1)}, s32[32]{0:T(128)}, u32[]{:S(2)}) copy-start(s32[32]{0:T(128)} %param.17) | copy-start | bytes 388
  129.5 41.8 %copy-start.5 = (bf16[52,3,1664]{2,0,1:T(8,128)(2,1)S(1)}, bf16[52,3,1664]{2,0,1:T(8,128)(2,1)}, u32[]{:S(2)}) copy-start(bf16[52,3,1664]{2,0,1:T(8,128)(2,1)} %param.29) | copy-start | bytes 1557508
  131.6 22.0 %all-to-all-start.1 = ((s32[32,4,1]{1,2,0:T(1,128)}), s32[32,4,1]{1,2,0:T(1,128)S(1)}, u32[]{:S(2)}, u32[]{:S(2)}) async-start(s32[32,4,1]{1,2,0:T(1,128)} %bitcast.3), calls=%async_computation.2 | async-start | bytes 32768 | tf_op jit(solution)/shard_map/all_to_all | solution.py:113
  177.6 7.7 %copy-start.6 = (f32[1664]{0:T(1024)S(1)}, f32[1664]{0:T(1024)}, u32[]{:S(2)}) copy-start(f32[1664]{0:T(1024)} %param.28) | copy-start | bytes 19972
  177.6 7.7 %copy-start.7 = (f32[1664]{0:T(1024)S(1)}, f32[1664]{0:T(1024)}, u32[]{:S(2)}) copy-start(f32[1664]{0:T(1024)} %param.27) | copy-start | bytes 19972
  177.6 233.4 %all-to-all-start.2 = ((bf16[32,52,3,1664]{3,1,2,0:T(8,128)(2,1)}), bf16[32,52,3,1664]{3,1,2,0:T(8,128)(2,1)}, u32[]{:S(2)}, u32[]{:S(2)}) async-start(bf16[32,52,3,1664]{3,1,2,0:T(8,128)(2,1)} %stack.2), calls=%async_computation.3 | async-start | bytes 35782656 | tf_op jit(solution)/shard_map/all_to_all | solution.py:61
  464.4 9.9 %copy-start.1 = (bf16[1024,1664]{1,0:T(8,128)(2,1)S(1)}, bf16[1024,1664]{1,0:T(8,128)(2,1)}, u32[]{:S(2)}) copy-start(bf16[1024,1664]{1,0:T(8,128)(2,1)} %param.24) | copy-start | bytes 10223620
Sparse Core Ops, SparseCore 0:
  32.2 82.4 all-reduce.1
  129.6 22.5 reduce-scatter.1
